TPU v7x, 512 devices: a whole 4x4x16 slice. The times are simulated.
512 devices in a mesh: gx: 16 (over z), gy: 4 (over x), gz: 8 (over y, core).
Axes of the slice: x: 4, y: 4, z: 16, core: 2. Of those that a mesh axis runs over, the one named last changes fastest.
Arguments:
- flow: float32 [4, 128, 64, 1024], P(None, 'gx', 'gy', 'gz'), may hold values from -3 to 3
- basis: float32 [127, 3, 131072], P(None, None, ('gx', 'gy', 'gz')), may hold values from -1150 to 1150
- sample: int32 [131072], P(('gx', 'gy', 'gz')), may hold values from 0 to 16383
Outputs:
- flow_next: float32 [4, 128, 64, 1024], P(None, 'gx', 'gy', 'gz')
- basis_next: float32 [128, 3, 131072], P(None, None, ('gx', 'gy', 'gz'))
- factor: float32 [128, 128], replicated
All inputs are finite; a program needn't handle non-finite values.
Results may differ from a plain program's by a relative error of at most 0.000065.
Values sent between devices are 32-bit elements; how exact they have to be, the bound alone decides.
A program may use at most 64 MiB of HBM per device.

v0:
```python
import jax
import jax.numpy as jnp
from jax import lax
from jax.sharding import PartitionSpec as P

DT_STEP = 0.35
VISCOSITY = 0.2
SOUND_SQ = 1.0
DRIVING = 0.5


def padded(block, sides, width, periodic):
    for axis, dim in sides:
        count = lax.axis_size(axis)
        forward = [(i, i + 1) for i in range(count - 1)]
        if periodic:
            forward.append((count - 1, 0))
        backward = [(target, source) for source, target in forward]
        low = lax.ppermute(
            lax.slice_in_dim(block, block.shape[dim] - width, None, axis=dim), axis, forward
        )
        high = lax.ppermute(lax.slice_in_dim(block, 0, width, axis=dim), axis, backward)
        block = jnp.concatenate([low, block, high], axis=dim)
    return block


def rates(ext):
    centre = ext[:, 1:-1, 1:-1, 1:-1]
    x_plus = ext[:, 2:, 1:-1, 1:-1]
    x_minus = ext[:, :-2, 1:-1, 1:-1]
    y_plus = ext[:, 1:-1, 2:, 1:-1]
    y_minus = ext[:, 1:-1, :-2, 1:-1]
    z_plus = ext[:, 1:-1, 1:-1, 2:]
    z_minus = ext[:, 1:-1, 1:-1, :-2]
    slope_x = 0.5 * (x_plus - x_minus)
    slope_y = 0.5 * (y_plus - y_minus)
    slope_z = 0.5 * (z_plus - z_minus)
    laplace = x_plus + x_minus + (y_plus + y_minus) + (z_plus + z_minus) - 6.0 * centre
    advect = centre[0] * slope_x[:3] + centre[1] * slope_y[:3] + centre[2] * slope_z[:3]
    pressure = jnp.stack([slope_x[3], slope_y[3], slope_z[3]])
    forcing = jnp.array([DRIVING, 0.0, 0.0], dtype=jnp.float32).reshape(3, 1, 1, 1)
    velocity = VISCOSITY * laplace[:3] - advect - pressure + forcing
    density = -SOUND_SQ * (slope_x[0] + slope_y[1] + slope_z[2])
    return jnp.concatenate([velocity, density[None]], axis=0)


def extend_one(fields):
    walled = padded(fields, (("gy", 2),), 1, False)
    return padded(walled, (("gx", 1), ("gz", 3)), 1, True)


def local(flow, basis, sample):
    points = basis.shape[2]
    modes = basis.shape[0]
    count = 3.0 * points * lax.axis_size("gx") * lax.axis_size("gy") * lax.axis_size("gz")
    section_one = flow + DT_STEP * rates(extend_one(flow))
    section_two = 0.75 * flow + 0.25 * (section_one + DT_STEP * rates(extend_one(section_one)))
    flow_next = 1.0 / 3.0 * flow + 2.0 / 3.0 * (
        section_two + DT_STEP * rates(extend_one(section_two))
    )
    velocity = flow_next[:3].reshape(3, -1)
    snapshot = jnp.take(velocity, sample, axis=1)
    stacked = jnp.concatenate([basis, snapshot[None]], axis=0).reshape(modes + 1, 3 * points)
    local_gram = jnp.dot(
        stacked, stacked.T, precision=lax.Precision.HIGHEST, preferred_element_type=jnp.float32
    )
    gram = lax.psum(local_gram, ("gx", "gy", "gz")) / count
    lower = jnp.linalg.cholesky(gram)
    basis_next = jax.scipy.linalg.solve_triangular(lower, stacked, lower=True).reshape(
        modes + 1, 3, points
    )
    return (flow_next, basis_next, lower.T)


def solution(mesh):
    return jax.shard_map(
        local,
        mesh=mesh,
        in_specs=(
            P(None, "gx", "gy", "gz"),
            P(None, None, ("gx", "gy", "gz")),
            P(("gx", "gy", "gz")),
        ),
        out_specs=(P(None, "gx", "gy", "gz"), P(None, None, ("gx", "gy", "gz")), P()),
        check_vma=False,
    )
```

profile of v0, /device:TPU:1, one launch (start us, length us, event | category | flops | bytes accessed | tf_op | source)
XLA Modules:
  0.0 582.4 jit_solution(7620865436270588193)
XLA Ops:
  8.3 3.9 collective-permute-start
  12.2 1.3 collective-permute-start.1
  14.4 2.2 collective-permute-done.1
  17.5 11.1 %collective-permute-start.2 = (f32[4,1,18,128]{3,2,1,0:T(8,128)S(1)}, f32[4,1,18,128]{3,2,1,0:T(8,128)S(1)}, u32[]{:S(2)}, u32[]{:S(2)}) collective-permute-start(f32[4,1,18,128]{3,2,1,0:T(8,128)S(1)} %get-tuple-element.41), channel_id=1, source_target_pairs={{32,0},{64,32},{96,64},{128,96},{160,128},{192,160},{224,192},{256... | collective-permute-start | bytes 110600 | tf_op jit(solution)/shard_map/ppermute | solution.py:22
  28.6 1.9 collective-permute-start.3
  31.2 3.4 collective-permute-done.3
  35.9 3.5 collective-permute-start.4
  40.6 1.6 subtract_multiply_fusion.5
  42.2 5.2 collective-permute-done.4
  47.4 1.4 subtract_multiply_fusion.4
  48.9 1.5 fusion.24
  50.4 3.1 collective-permute-start.6
  53.6 1.3 collective-permute-start.7
  54.9 3.1 collective-permute-done.7
  58.1 1.9 collective-permute-start.8
  60.0 3.4 collective-permute-start.9
  63.4 2.6 collective-permute-done.9
  66.3 4.2 collective-permute-start.10
  70.7 6.5 %collective-permute-done.10 = f32[4,10,18,1]{3,2,1,0:T(8,128)S(1)} collective-permute-done((f32[4,10,18,1]{3,2,1,0:T(8,128)S(1)}, f32[4,10,18,1]{3,2,1,0:T(8,128)S(1)}, u32[]{:S(2)}, u32[]{:S(2)}) %collective-permute-start.10) | collective-permute-done | bytes 2912 | tf_op jit(solution)/shard_map/ppermute | solution.py:22
  77.9 2.8 collective-permute-start.12
  80.7 1.3 collective-permute-start.13
  82.2 3.0 collective-permute-done.13
  85.2 1.9 collective-permute-start.14
  87.1 3.5 collective-permute-start.15
  90.7 2.5 collective-permute-done.15
  93.4 5.4 collective-permute-start.16
  99.0 5.4 collective-permute-done.16
  105.3 4.7 copy.16
  110.1 4.1 gather_fusion
  115.8 433.0 %all-reduce.2.cloned.1.call-done = f32[128,128]{0,1:T(8,128)} async-done(((f32[128,128]{0,1:T(8,128)}), f32[128,128]{0,1:T(8,128)}) %all-reduce.2.cloned.1.call-update) | async-done | bytes 65552 | tf_op jit(solution)/shard_map/psum | solution.py:67
  550.6 11.7 %cholesky.16 = f32[128,128]{1,0:T(8,128)S(1)} custom-call(f32[128,128]{1,0:T(8,128)S(1)} %fusion.57), custom_call_target="Cholesky" | custom-call | tf_op jit(solution)/shard_map/jit(cholesky)/cholesky | solution.py:68
  563.7 9.8 %custom-call.7 = f32[1,128,128]{1,2,0:T(8,128)S(1)} custom-call(f32[1,128,128]{2,1,0:T(8,128)S(1)} %get-tuple-element.70), custom_call_target="InvertDiagBlocksLowerTriangular" | custom-call | tf_op jit(solution)/shard_map/jit(_solve_triangular)/triangular_solve | solution.py:69
  (71 shorter events, 15.2 us)
Async XLA Ops:
  7.2 43.2 %copy-start = (f32[4,8,16,128]{3,2,1,0:T(8,128)S(1)}, f32[4,8,16,128]{3,2,1,0:T(8,128)}, u32[]{:S(2)}) copy-start(f32[4,8,16,128]{3,2,1,0:T(8,128)} %param.6) | copy-start | bytes 786436
  7.2 47.7 %copy-start.4 = (s32[256]{0:T(256)S(1)}, s32[256]{0:T(256)}, u32[]{:S(2)}) copy-start(s32[256]{0:T(256)} %param.8) | copy-start | bytes 3076
  7.2 541.6 %all-reduce.2.cloned.1.call-start = ((), (), s32[]{:S(2)}) async-start(), calls=%async_computation | async-start | bytes 131072 | tf_op jit(solution)/shard_map/psum | solution.py:67
  8.3 6.2 %collective-permute-start = (f32[4,8,1,128]{3,2,1,0:T(1,128)S(1)}, f32[4,8,1,128]{3,2,1,0:T(1,128)S(1)}, u32[]{:S(2)}, u32[]{:S(2)}) collective-permute-start(f32[4,8,1,128]{3,2,1,0:T(1,128)S(1)} %get-tuple-element.67), channel_id=1, source_target_pairs={{0,8},{8,16},{16,24},{1,9},{9,17},{17,25},{2,10},{10,18},{18,26},{... | collective-permute-start | bytes 49160 | tf_op jit(solution)/shard_map/ppermute | solution.py:19
  12.2 4.5 collective-permute-start.1
  17.5 13.7 %collective-permute-start.2 = (f32[4,1,18,128]{3,2,1,0:T(8,128)S(1)}, f32[4,1,18,128]{3,2,1,0:T(8,128)S(1)}, u32[]{:S(2)}, u32[]{:S(2)}) collective-permute-start(f32[4,1,18,128]{3,2,1,0:T(8,128)S(1)} %get-tuple-element.41), channel_id=1, source_target_pairs={{32,0},{64,32},{96,64},{128,96},{160,128},{192,160},{224,192},{256... | collective-permute-start | bytes 110600 | tf_op jit(solution)/shard_map/ppermute | solution.py:22
  28.6 6.0 %collective-permute-start.3 = (f32[4,1,18,128]{3,2,1,0:T(8,128)S(1)}, f32[4,1,18,128]{3,2,1,0:T(8,128)S(1)}, u32[]{:S(2)}, u32[]{:S(2)}) collective-permute-start(f32[4,1,18,128]{3,2,1,0:T(8,128)S(1)} %get-tuple-element.40), channel_id=1, source_target_pairs={{0,32},{32,64},{64,96},{96,128},{128,160},{160,192},{192,224},{224... | collective-permute-start | bytes 110600 | tf_op jit(solution)/shard_map/ppermute | solution.py:19
  35.7 41.9 %copy-start.3 = (f32[3]{0:T(128)S(1)}, f32[3]{0:T(128)}, u32[]{:S(2)}) copy-start(f32[3]{0:T(128)} %constant.80.clone) | copy-start | bytes 40
  35.9 11.5 %collective-permute-start.4 = (f32[4,10,18,1]{3,2,1,0:T(8,128)S(1)}, f32[4,10,18,1]{3,2,1,0:T(8,128)S(1)}, u32[]{:S(2)}, u32[]{:S(2)}) collective-permute-start(f32[4,10,18,1]{3,2,1,0:T(8,128)S(1)} %get-tuple-element.31), channel_id=1, source_target_pairs={{1,0},{2,1},{3,2},{4,3},{5,4},{6,5},{7,6},{0,7},{9,8},{10,9},{11,1... | collective-permute-start | bytes 8648 | tf_op jit(solution)/shard_map/ppermute | solution.py:22
  39.4 8.0 %collective-permute-start.5 = (f32[4,10,18,1]{3,2,1,0:T(8,128)S(1)}, f32[4,10,18,1]{3,2,1,0:T(8,128)S(1)}, u32[]{:S(2)}, u32[]{:S(2)}) collective-permute-start(f32[4,10,18,1]{3,2,1,0:T(8,128)S(1)} %get-tuple-element.32), channel_id=1, source_target_pairs={{0,1},{1,2},{2,3},{3,4},{4,5},{5,6},{6,7},{7,0},{8,9},{9,10},{10,1... | collective-permute-start | bytes 8648 | tf_op jit(solution)/shard_map/ppermute | solution.py:19
  42.2 39.8 %copy-start.1 = (f32[127,3,256]{2,0,1:T(8,128)S(1)}, f32[127,3,256]{2,0,1:T(8,128)}, u32[]{:S(2)}) copy-start(f32[127,3,256]{2,0,1:T(8,128)} %param.7) | copy-start | bytes 1170436
  50.4 4.5 collective-permute-start.6
  53.6 4.5 collective-permute-start.7
  58.1 5.3 collective-permute-start.8
  60.0 6.0 %collective-permute-start.9 = (f32[4,1,18,128]{3,2,1,0:T(8,128)S(1)}, f32[4,1,18,128]{3,2,1,0:T(8,128)S(1)}, u32[]{:S(2)}, u32[]{:S(2)}) collective-permute-start(f32[4,1,18,128]{3,2,1,0:T(8,128)S(1)} %get-tuple-element.37), channel_id=1, source_target_pairs={{0,32},{32,64},{64,96},{96,128},{128,160},{160,192},{192,224},{224... | collective-permute-start | bytes 110600 | tf_op jit(solution)/shard_map/ppermute | solution.py:19
  66.3 10.9 %collective-permute-start.10 = (f32[4,10,18,1]{3,2,1,0:T(8,128)S(1)}, f32[4,10,18,1]{3,2,1,0:T(8,128)S(1)}, u32[]{:S(2)}, u32[]{:S(2)}) collective-permute-start(f32[4,10,18,1]{3,2,1,0:T(8,128)S(1)} %get-tuple-element.29), channel_id=1, source_target_pairs={{1,0},{2,1},{3,2},{4,3},{5,4},{6,5},{7,6},{0,7},{9,8},{10,9},{11,1... | collective-permute-start | bytes 8648 | tf_op jit(solution)/shard_map/ppermute | solution.py:22
  70.5 6.6 %collective-permute-start.11 = (f32[4,10,18,1]{3,2,1,0:T(8,128)S(1)}, f32[4,10,18,1]{3,2,1,0:T(8,128)S(1)}, u32[]{:S(2)}, u32[]{:S(2)}) collective-permute-start(f32[4,10,18,1]{3,2,1,0:T(8,128)S(1)} %get-tuple-element.30), channel_id=1, source_target_pairs={{0,1},{1,2},{2,3},{3,4},{4,5},{5,6},{6,7},{7,0},{8,9},{9,10},{10,1... | collective-permute-start | bytes 8648 | tf_op jit(solution)/shard_map/ppermute | solution.py:19
  77.9 4.3 collective-permute-start.12
  80.7 4.5 collective-permute-start.13
  85.2 5.5 collective-permute-start.14
  87.1 6.0 %collective-permute-start.15 = (f32[4,1,18,128]{3,2,1,0:T(8,128)S(1)}, f32[4,1,18,128]{3,2,1,0:T(8,128)S(1)}, u32[]{:S(2)}, u32[]{:S(2)}) collective-permute-start(f32[4,1,18,128]{3,2,1,0:T(8,128)S(1)} %get-tuple-element.34), channel_id=1, source_target_pairs={{0,32},{32,64},{64,96},{96,128},{128,160},{160,192},{192,224},{224... | collective-permute-start | bytes 110600 | tf_op jit(solution)/shard_map/ppermute | solution.py:19
  93.4 11.0 %collective-permute-start.16 = (f32[4,10,18,1]{3,2,1,0:T(8,128)S(1)}, f32[4,10,18,1]{3,2,1,0:T(8,128)S(1)}, u32[]{:S(2)}, u32[]{:S(2)}) collective-permute-start(f32[4,10,18,1]{3,2,1,0:T(8,128)S(1)} %get-tuple-element.27), channel_id=1, source_target_pairs={{1,0},{2,1},{3,2},{4,3},{5,4},{6,5},{7,6},{0,7},{9,8},{10,9},{11,1... | collective-permute-start | bytes 8648 | tf_op jit(solution)/shard_map/ppermute | solution.py:22
  98.9 5.8 collective-permute-start.17
  105.3 470.2 %copy-start.2 = (f32[4,8,16,128]{3,2,1,0:T(8,128)}, f32[4,8,16,128]{3,2,1,0:T(8,128)S(1)}, u32[]{:S(2)}) copy-start(f32[4,8,16,128]{3,2,1,0:T(8,128)S(1)} %fusion.15) | copy-start | bytes 786436
Sparse Core Ops, SparseCore 0:
  115.5 433.2 all-reduce.1
where the time goes:
time: 583 us; the launch traced here: 582 us
  waiting for transfers between devices  467 us (80%)
  starting transfers between devices  52 us (9%)
  other arithmetic  33.4 us (6%)
  between operations  14.5 us (2%)
  local copies, waits for them, and re-layouts  12.7 us (2%)
    psum x1, waiting for transfers between devices, local(): gram = lax.psum(local_gram, ('gx', 'gy', 'gz')) / count  433 us
    ppermute x9, starting transfers between devices, padded(): lax.ppermute(lax.slice_in_dim(block, 0, width, axis=dim), axis, backward)  32.1 us
    ppermute x9, waiting for transfers between devices, padded(): lax.ppermute(lax.slice_in_dim(block, 0, width, axis=dim), axis, backward)  25.5 us
    ppermute x9, starting transfers between devices, padded(): lax.ppermute(lax.slice_in_dim(block, block.shape[dim] - width, None, axis...  19.9 us
    another operation x3, other arithmetic, local(): lower = jnp.linalg.cholesky(gram)  12.4 us
  transfers between devices with their start and end apart: 19, of which 11 were waited for; matrix products, arithmetic and copies ran while one was open for 1% of the time, Pallas kernels for 0%

commit v1 on v0

--- a/solution.py
+++ b/solution.py
@@ -64,7 +64,7 @@
     local_gram = jnp.dot(
         stacked, stacked.T, precision=lax.Precision.HIGHEST, preferred_element_type=jnp.float32
     )
-    gram = lax.psum(local_gram, ("gx", "gy", "gz")) / count
+    gram = lax.psum(lax.psum(local_gram, ("gy", "gz")), "gx") / count
     lower = jnp.linalg.cholesky(gram)
     basis_next = jax.scipy.linalg.solve_triangular(lower, stacked, lower=True).reshape(
         modes + 1, 3, points

time: 583 us -> 403 us (0.69)
  the two profiles are of different devices: /device:TPU:1 before, /device:TPU:2 now
where the time goes in v1:
time: 403 us; the launch traced here: 402 us
  waiting for transfers between devices  293 us (73%)
  starting transfers between devices  46.1 us (11%)
  other arithmetic  33.4 us (8%)
  between operations  14.5 us (4%)
  local copies, waits for them, and re-layouts  12.7 us (3%)
    psum x2, waiting for transfers between devices, local(): gram = lax.psum(lax.psum(local_gram, ('gy', 'gz')), 'gx') / count  252 us
    ppermute x9, starting transfers between devices, padded(): lax.ppermute(lax.slice_in_dim(block, 0, width, axis=dim), axis, backward)  26.1 us
    ppermute x9, waiting for transfers between devices, padded(): lax.ppermute(lax.slice_in_dim(block, 0, width, axis=dim), axis, backward)  20.7 us
    ppermute x9, waiting for transfers between devices, padded(): lax.ppermute(lax.slice_in_dim(block, block.shape[dim] - width, None, axis...  20.4 us
    ppermute x9, starting transfers between devices, padded(): lax.ppermute(lax.slice_in_dim(block, block.shape[dim] - width, None, axis...  19.7 us
    another operation x3, other arithmetic, local(): lower = jnp.linalg.cholesky(gram)  12.4 us
    another operation x1, other arithmetic, local(): jax.scipy.linalg.solve_triangular(lower, stacked, lower=True)  9.81 us
  transfers between devices with their start and end apart: 20, of which 16 were waited for; matrix products, arithmetic and copies ran while one was open for 1% of the time, Pallas kernels for 0%

profile of v1, /device:TPU:2, one launch (start us, length us, event | category | flops | bytes accessed | tf_op | source)
XLA Modules:
  0.0 402.5 jit_solution(10307079722030106917)
XLA Ops:
  8.3 3.4 collective-permute-start
  11.7 5.7 %collective-permute-start.1 = (f32[4,8,1,128]{3,2,1,0:T(1,128)S(1)}, f32[4,8,1,128]{3,2,1,0:T(1,128)S(1)}, u32[]{:S(2)}, u32[]{:S(2)}) collective-permute-start(f32[4,8,1,128]{3,2,1,0:T(1,128)S(1)} %get-tuple-element.68), channel_id=1, source_target_pairs={{8,0},{16,8},{24,16},{9,1},{17,9},{25,17},{10,2},{18,10},{26,18},{... | collective-permute-start | bytes 49160 | tf_op jit(solution)/shard_map/ppermute | solution.py:22
  19.6 9.9 %collective-permute-start.2 = (f32[4,1,18,128]{3,2,1,0:T(8,128)S(1)}, f32[4,1,18,128]{3,2,1,0:T(8,128)S(1)}, u32[]{:S(2)}, u32[]{:S(2)}) collective-permute-start(f32[4,1,18,128]{3,2,1,0:T(8,128)S(1)} %get-tuple-element.41), channel_id=1, source_target_pairs={{32,0},{64,32},{96,64},{128,96},{160,128},{192,160},{224,192},{256... | collective-permute-start | bytes 110600 | tf_op jit(solution)/shard_map/ppermute | solution.py:22
  29.5 1.9 collective-permute-start.3
  32.1 4.6 %collective-permute-done.3 = f32[4,1,18,128]{3,2,1,0:T(8,128)S(1)} collective-permute-done((f32[4,1,18,128]{3,2,1,0:T(8,128)S(1)}, f32[4,1,18,128]{3,2,1,0:T(8,128)S(1)}, u32[]{:S(2)}, u32[]{:S(2)}) %collective-permute-start.3) | collective-permute-done | bytes 36896 | tf_op jit(solution)/shard_map/ppermute | solution.py:19
  38.4 1.6 subtract_multiply_fusion.5
  40.0 4.3 %collective-permute-done.4 = f32[4,10,18,1]{3,2,1,0:T(8,128)S(1)} collective-permute-done((f32[4,10,18,1]{3,2,1,0:T(8,128)S(1)}, f32[4,10,18,1]{3,2,1,0:T(8,128)S(1)}, u32[]{:S(2)}, u32[]{:S(2)}) %collective-permute-start.4) | collective-permute-done | bytes 2912 | tf_op jit(solution)/shard_map/ppermute | solution.py:22
  44.3 3.3 collective-permute-done.5
  47.6 1.4 subtract_multiply_fusion.4
  49.0 1.5 fusion.24
  50.6 3.1 collective-permute-start.6
  53.7 2.7 collective-permute-start.7
  56.5 2.9 collective-permute-done.7
  59.4 1.9 collective-permute-start.8
  61.3 3.9 collective-permute-start.9
  65.3 3.1 collective-permute-done.9
  69.4 5.7 %collective-permute-done.10 = f32[4,10,18,1]{3,2,1,0:T(8,128)S(1)} collective-permute-done((f32[4,10,18,1]{3,2,1,0:T(8,128)S(1)}, f32[4,10,18,1]{3,2,1,0:T(8,128)S(1)}, u32[]{:S(2)}, u32[]{:S(2)}) %collective-permute-start.10) | collective-permute-done | bytes 2912 | tf_op jit(solution)/shard_map/ppermute | solution.py:22
  75.1 3.1 collective-permute-done.11
  78.9 1.9 collective-permute-start.12
  80.9 3.9 collective-permute-start.13
  85.0 1.5 collective-permute-done.13
  86.5 1.9 collective-permute-start.14
  88.4 3.9 collective-permute-start.15
  92.5 3.1 collective-permute-done.15
  96.5 5.7 %collective-permute-done.16 = f32[4,10,18,1]{3,2,1,0:T(8,128)S(1)} collective-permute-done((f32[4,10,18,1]{3,2,1,0:T(8,128)S(1)}, f32[4,10,18,1]{3,2,1,0:T(8,128)S(1)}, u32[]{:S(2)}, u32[]{:S(2)}) %collective-permute-start.16) | collective-permute-done | bytes 2912 | tf_op jit(solution)/shard_map/ppermute | solution.py:22
  102.3 3.1 collective-permute-done.17
  106.1 4.7 %copy.16 = f32[3,8,16,128]{0,3,2,1:T(8,128)} copy(f32[3,8,16,128]{3,2,1,0:T(8,128)S(1)} %slice.406) | data formatting | bytes 393216 | tf_op jit(solution)/shard_map/slice | solution.py:61
  110.8 4.1 %gather_fusion = f32[256,3]{1,0:T(8,128)S(1)} fusion(f32[3,16384]{0,1:T(8,128)} %bitcast.47, s32[1024]{0:T(1024)S(1)} %pad_clamp_fusion), kind=kCustom, calls=%fused_computation | custom fusion | bytes 7168 | tf_op jit(solution)/shard_map/jit(_take)/gather | solution.py:62
  116.6 116.8 %all-reduce.3.cloned.1.call-done = f32[128,128]{0,1:T(8,128)} async-done(((f32[128,128]{0,1:T(8,128)}), f32[128,128]{0,1:T(8,128)}) %all-reduce.3.cloned.1.call-update) | async-done | bytes 65552 | tf_op jit(solution)/shard_map/psum | solution.py:67
  233.6 135.4 %all-reduce.5.cloned.1.call-done = f32[128,128]{0,1:T(8,128)} async-done(((f32[128,128]{0,1:T(8,128)}), f32[128,128]{0,1:T(8,128)}) %all-reduce.5.cloned.1.call-update) | async-done | bytes 65552 | tf_op jit(solution)/shard_map/psum | solution.py:67
  370.8 11.7 %cholesky.16 = f32[128,128]{1,0:T(8,128)S(1)} custom-call(f32[128,128]{1,0:T(8,128)S(1)} %fusion.57), custom_call_target="Cholesky" | custom-call | tf_op jit(solution)/shard_map/jit(cholesky)/cholesky | solution.py:68
  383.8 9.8 %custom-call.7 = f32[1,128,128]{1,2,0:T(8,128)S(1)} custom-call(f32[1,128,128]{2,1,0:T(8,128)S(1)} %get-tuple-element.70), custom_call_target="InvertDiagBlocksLowerTriangular" | custom-call | tf_op jit(solution)/shard_map/jit(_solve_triangular)/triangular_solve | solution.py:69
  (74 shorter events, 16.3 us)
Async XLA Ops:
  7.2 43.3 %copy-start = (f32[4,8,16,128]{3,2,1,0:T(8,128)S(1)}, f32[4,8,16,128]{3,2,1,0:T(8,128)}, u32[]{:S(2)}) copy-start(f32[4,8,16,128]{3,2,1,0:T(8,128)} %param.6) | copy-start | bytes 786436
  7.2 49.3 %copy-start.4 = (s32[256]{0:T(256)S(1)}, s32[256]{0:T(256)}, u32[]{:S(2)}) copy-start(s32[256]{0:T(256)} %param.8) | copy-start | bytes 3076
  7.2 226.2 %all-reduce.3.cloned.1.call-start = ((), (), s32[]{:S(2)}) async-start(), calls=%async_computation | async-start | bytes 131072 | tf_op jit(solution)/shard_map/psum | solution.py:67
  8.3 10.0 %collective-permute-start = (f32[4,8,1,128]{3,2,1,0:T(1,128)S(1)}, f32[4,8,1,128]{3,2,1,0:T(1,128)S(1)}, u32[]{:S(2)}, u32[]{:S(2)}) collective-permute-start(f32[4,8,1,128]{3,2,1,0:T(1,128)S(1)} %get-tuple-element.67), channel_id=1, source_target_pairs={{0,8},{8,16},{16,24},{1,9},{9,17},{17,25},{2,10},{10,18},{18,26},{... | collective-permute-start | bytes 49160 | tf_op jit(solution)/shard_map/ppermute | solution.py:19
  11.7 7.1 %collective-permute-start.1 = (f32[4,8,1,128]{3,2,1,0:T(1,128)S(1)}, f32[4,8,1,128]{3,2,1,0:T(1,128)S(1)}, u32[]{:S(2)}, u32[]{:S(2)}) collective-permute-start(f32[4,8,1,128]{3,2,1,0:T(1,128)S(1)} %get-tuple-element.68), channel_id=1, source_target_pairs={{8,0},{16,8},{24,16},{9,1},{17,9},{25,17},{10,2},{18,10},{26,18},{... | collective-permute-start | bytes 49160 | tf_op jit(solution)/shard_map/ppermute | solution.py:22
  19.6 12.5 %collective-permute-start.2 = (f32[4,1,18,128]{3,2,1,0:T(8,128)S(1)}, f32[4,1,18,128]{3,2,1,0:T(8,128)S(1)}, u32[]{:S(2)}, u32[]{:S(2)}) collective-permute-start(f32[4,1,18,128]{3,2,1,0:T(8,128)S(1)} %get-tuple-element.41), channel_id=1, source_target_pairs={{32,0},{64,32},{96,64},{128,96},{160,128},{192,160},{224,192},{256... | collective-permute-start | bytes 110600 | tf_op jit(solution)/shard_map/ppermute | solution.py:22
  29.5 7.2 %collective-permute-start.3 = (f32[4,1,18,128]{3,2,1,0:T(8,128)S(1)}, f32[4,1,18,128]{3,2,1,0:T(8,128)S(1)}, u32[]{:S(2)}, u32[]{:S(2)}) collective-permute-start(f32[4,1,18,128]{3,2,1,0:T(8,128)S(1)} %get-tuple-element.40), channel_id=1, source_target_pairs={{0,32},{32,64},{64,96},{96,128},{128,160},{160,192},{192,224},{224... | collective-permute-start | bytes 110600 | tf_op jit(solution)/shard_map/ppermute | solution.py:19
  37.7 40.9 %copy-start.3 = (f32[3]{0:T(128)S(1)}, f32[3]{0:T(128)}, u32[]{:S(2)}) copy-start(f32[3]{0:T(128)} %constant.80.clone) | copy-start | bytes 40
  37.9 6.4 %collective-permute-start.4 = (f32[4,10,18,1]{3,2,1,0:T(8,128)S(1)}, f32[4,10,18,1]{3,2,1,0:T(8,128)S(1)}, u32[]{:S(2)}, u32[]{:S(2)}) collective-permute-start(f32[4,10,18,1]{3,2,1,0:T(8,128)S(1)} %get-tuple-element.31), channel_id=1, source_target_pairs={{1,0},{2,1},{3,2},{4,3},{5,4},{6,5},{7,6},{0,7},{9,8},{10,9},{11,1... | collective-permute-start | bytes 8648 | tf_op jit(solution)/shard_map/ppermute | solution.py:22
  37.9 9.6 %collective-permute-start.5 = (f32[4,10,18,1]{3,2,1,0:T(8,128)S(1)}, f32[4,10,18,1]{3,2,1,0:T(8,128)S(1)}, u32[]{:S(2)}, u32[]{:S(2)}) collective-permute-start(f32[4,10,18,1]{3,2,1,0:T(8,128)S(1)} %get-tuple-element.32), channel_id=1, source_target_pairs={{0,1},{1,2},{2,3},{3,4},{4,5},{5,6},{6,7},{7,0},{8,9},{9,10},{10,1... | collective-permute-start | bytes 8648 | tf_op jit(solution)/shard_map/ppermute | solution.py:19
  40.0 44.8 %copy-start.1 = (f32[127,3,256]{2,0,1:T(8,128)S(1)}, f32[127,3,256]{2,0,1:T(8,128)}, u32[]{:S(2)}) copy-start(f32[127,3,256]{2,0,1:T(8,128)} %param.7) | copy-start | bytes 1170436
  50.6 5.9 %collective-permute-start.6 = (f32[4,8,1,128]{3,2,1,0:T(1,128)S(1)}, f32[4,8,1,128]{3,2,1,0:T(1,128)S(1)}, u32[]{:S(2)}, u32[]{:S(2)}) collective-permute-start(f32[4,8,1,128]{3,2,1,0:T(1,128)S(1)} %get-tuple-element.58), channel_id=1, source_target_pairs={{0,8},{8,16},{16,24},{1,9},{9,17},{17,25},{2,10},{10,18},{18,26},{... | collective-permute-start | bytes 49160 | tf_op jit(solution)/shard_map/ppermute | solution.py:19
  53.7 5.6 %collective-permute-start.7 = (f32[4,8,1,128]{3,2,1,0:T(1,128)S(1)}, f32[4,8,1,128]{3,2,1,0:T(1,128)S(1)}, u32[]{:S(2)}, u32[]{:S(2)}) collective-permute-start(f32[4,8,1,128]{3,2,1,0:T(1,128)S(1)} %get-tuple-element.59), channel_id=1, source_target_pairs={{8,0},{16,8},{24,16},{9,1},{17,9},{25,17},{10,2},{18,10},{26,18},{... | collective-permute-start | bytes 49160 | tf_op jit(solution)/shard_map/ppermute | solution.py:22
  59.4 6.0 %collective-permute-start.8 = (f32[4,1,18,128]{3,2,1,0:T(8,128)S(1)}, f32[4,1,18,128]{3,2,1,0:T(8,128)S(1)}, u32[]{:S(2)}, u32[]{:S(2)}) collective-permute-start(f32[4,1,18,128]{3,2,1,0:T(8,128)S(1)} %get-tuple-element.38), channel_id=1, source_target_pairs={{32,0},{64,32},{96,64},{128,96},{160,128},{192,160},{224,192},{256... | collective-permute-start | bytes 110600 | tf_op jit(solution)/shard_map/ppermute | solution.py:22
  61.3 7.2 %collective-permute-start.9 = (f32[4,1,18,128]{3,2,1,0:T(8,128)S(1)}, f32[4,1,18,128]{3,2,1,0:T(8,128)S(1)}, u32[]{:S(2)}, u32[]{:S(2)}) collective-permute-start(f32[4,1,18,128]{3,2,1,0:T(8,128)S(1)} %get-tuple-element.37), channel_id=1, source_target_pairs={{0,32},{32,64},{64,96},{96,128},{128,160},{160,192},{192,224},{224... | collective-permute-start | bytes 110600 | tf_op jit(solution)/shard_map/ppermute | solution.py:19
  68.7 6.4 %collective-permute-start.10 = (f32[4,10,18,1]{3,2,1,0:T(8,128)S(1)}, f32[4,10,18,1]{3,2,1,0:T(8,128)S(1)}, u32[]{:S(2)}, u32[]{:S(2)}) collective-permute-start(f32[4,10,18,1]{3,2,1,0:T(8,128)S(1)} %get-tuple-element.29), channel_id=1, source_target_pairs={{1,0},{2,1},{3,2},{4,3},{5,4},{6,5},{7,6},{0,7},{9,8},{10,9},{11,1... | collective-permute-start | bytes 8648 | tf_op jit(solution)/shard_map/ppermute | solution.py:22
  68.8 9.5 %collective-permute-start.11 = (f32[4,10,18,1]{3,2,1,0:T(8,128)S(1)}, f32[4,10,18,1]{3,2,1,0:T(8,128)S(1)}, u32[]{:S(2)}, u32[]{:S(2)}) collective-permute-start(f32[4,10,18,1]{3,2,1,0:T(8,128)S(1)} %get-tuple-element.30), channel_id=1, source_target_pairs={{0,1},{1,2},{2,3},{3,4},{4,5},{5,6},{6,7},{7,0},{8,9},{9,10},{10,1... | collective-permute-start | bytes 8648 | tf_op jit(solution)/shard_map/ppermute | solution.py:19
  78.9 6.1 %collective-permute-start.12 = (f32[4,8,1,128]{3,2,1,0:T(1,128)S(1)}, f32[4,8,1,128]{3,2,1,0:T(1,128)S(1)}, u32[]{:S(2)}, u32[]{:S(2)}) collective-permute-start(f32[4,8,1,128]{3,2,1,0:T(1,128)S(1)} %get-tuple-element.49), channel_id=1, source_target_pairs={{0,8},{8,16},{16,24},{1,9},{9,17},{17,25},{2,10},{10,18},{18,26},{... | collective-permute-start | bytes 49160 | tf_op jit(solution)/shard_map/ppermute | solution.py:19
  80.9 5.6 %collective-permute-start.13 = (f32[4,8,1,128]{3,2,1,0:T(1,128)S(1)}, f32[4,8,1,128]{3,2,1,0:T(1,128)S(1)}, u32[]{:S(2)}, u32[]{:S(2)}) collective-permute-start(f32[4,8,1,128]{3,2,1,0:T(1,128)S(1)} %get-tuple-element.50), channel_id=1, source_target_pairs={{8,0},{16,8},{24,16},{9,1},{17,9},{25,17},{10,2},{18,10},{26,18},{... | collective-permute-start | bytes 49160 | tf_op jit(solution)/shard_map/ppermute | solution.py:22
  86.5 6.0 %collective-permute-start.14 = (f32[4,1,18,128]{3,2,1,0:T(8,128)S(1)}, f32[4,1,18,128]{3,2,1,0:T(8,128)S(1)}, u32[]{:S(2)}, u32[]{:S(2)}) collective-permute-start(f32[4,1,18,128]{3,2,1,0:T(8,128)S(1)} %get-tuple-element.35), channel_id=1, source_target_pairs={{32,0},{64,32},{96,64},{128,96},{160,128},{192,160},{224,192},{256... | collective-permute-start | bytes 110600 | tf_op jit(solution)/shard_map/ppermute | solution.py:22
  88.4 7.2 %collective-permute-start.15 = (f32[4,1,18,128]{3,2,1,0:T(8,128)S(1)}, f32[4,1,18,128]{3,2,1,0:T(8,128)S(1)}, u32[]{:S(2)}, u32[]{:S(2)}) collective-permute-start(f32[4,1,18,128]{3,2,1,0:T(8,128)S(1)} %get-tuple-element.34), channel_id=1, source_target_pairs={{0,32},{32,64},{64,96},{96,128},{128,160},{160,192},{192,224},{224... | collective-permute-start | bytes 110600 | tf_op jit(solution)/shard_map/ppermute | solution.py:19
  95.9 6.4 %collective-permute-start.16 = (f32[4,10,18,1]{3,2,1,0:T(8,128)S(1)}, f32[4,10,18,1]{3,2,1,0:T(8,128)S(1)}, u32[]{:S(2)}, u32[]{:S(2)}) collective-permute-start(f32[4,10,18,1]{3,2,1,0:T(8,128)S(1)} %get-tuple-element.27), channel_id=1, source_target_pairs={{1,0},{2,1},{3,2},{4,3},{5,4},{6,5},{7,6},{0,7},{9,8},{10,9},{11,1... | collective-permute-start | bytes 8648 | tf_op jit(solution)/shard_map/ppermute | solution.py:22
  95.9 9.5 %collective-permute-start.17 = (f32[4,10,18,1]{3,2,1,0:T(8,128)S(1)}, f32[4,10,18,1]{3,2,1,0:T(8,128)S(1)}, u32[]{:S(2)}, u32[]{:S(2)}) collective-permute-start(f32[4,10,18,1]{3,2,1,0:T(8,128)S(1)} %get-tuple-element.28), channel_id=1, source_target_pairs={{0,1},{1,2},{2,3},{3,4},{4,5},{5,6},{6,7},{7,0},{8,9},{9,10},{10,1... | collective-permute-start | bytes 8648 | tf_op jit(solution)/shard_map/ppermute | solution.py:19
  106.0 289.6 %copy-start.2 = (f32[4,8,16,128]{3,2,1,0:T(8,128)}, f32[4,8,16,128]{3,2,1,0:T(8,128)S(1)}, u32[]{:S(2)}) copy-start(f32[4,8,16,128]{3,2,1,0:T(8,128)S(1)} %fusion.15) | copy-start | bytes 786436
  116.1 252.8 %all-reduce.5.cloned.1.call-start = ((), (), s32[]{:S(2)}) async-start(), calls=%async_computation.1 | async-start | bytes 131072 | tf_op jit(solution)/shard_map/psum | solution.py:67
Sparse Core Ops, SparseCore 0:
  116.2 117.0 all-reduce.2
  235.8 133.1 all-reduce.4
